TPU v7x, 256 devices: a whole 4x4x8 slice. The times are simulated.
256 devices in a mesh: grp: 2 (over core), fsdp: 16 (over y, z_lo), tp: 8 (over x, z_hi).
Axes of the slice: x: 4, y: 4, z: 8 (z_hi: 2, z_lo: 4; z = z_hi * 4 + z_lo), core: 2. Of those that a mesh axis runs over, the one named last changes fastest.
Arguments:
- frames: bfloat16 [2, 4096, 8192], P('grp', 'fsdp'), may hold values from -6 to 6
- rewards: bfloat16 [4096], P('fsdp'), may hold values from -5 to 5
- actions: int32 [2, 4096], P('grp', 'fsdp'), may hold values from 0 to 17
- fractions: int32 [2, 4096, 32], P('grp', 'fsdp'), may hold values from 0 to 63
- episode_shard: int32 [4096, 1], P('fsdp'), may hold values from 0 to 15, as said below
- table: float32 [64], replicated, may hold values from 0.02 to 0.98
- norm_gain: float32 [8192], replicated, may hold values from 0.1 to 1.9
- torso_weight: bfloat16 [8192, 4096], P(('grp', 'fsdp'), 'tp'), may hold values from -0.0625 to 0.0625
- embed_weight: bfloat16 [64, 4096], P(None, 'tp'), may hold values from -0.75 to 0.75
- value_weight: bfloat16 [18, 4096], P(None, 'tp'), may hold values from -0.59765625 to 0.59765625
Outputs:
- torso_grad: float32 [8192, 4096], P(('grp', 'fsdp'), 'tp')
- refreshed_weight: bfloat16 [8192, 4096], P(('grp', 'fsdp', 'tp'))
Inputs may be any that keep to these rules, and one draw needn't show every extreme that they name: `episode_shard`: of the rows of one index of fsdp, at most 24 belong to one learner shard, and in every such block some learner shard gets exactly 24; every learner shard gets at least one row from every block.
All inputs are finite; a program needn't handle non-finite values.
Results may differ from a plain program's by a relative error of at most 0.0075.
Values may be sent and summed in bfloat16 or wider, within the bound.
No kernel may reach another device: no remote copies, remote signals or barrier semaphores. Data moves between devices by JAX's collectives and lax.ppermute only.
A program may use at most 64 MiB of HBM per device.

v0:
```python
import jax
import jax.numpy as jnp
from jax import lax
from jax.sharding import PartitionSpec as P

ACTIONS = 18
COSINES = 64
FRACS = 64


def shards(
    frames,
    rewards,
    actions,
    fractions,
    episode_shard,
    table,
    norm_gain,
    torso_weight,
    embed_weight,
    value_weight,
):
    shard_total = lax.axis_size("fsdp")
    destination = episode_shard[:, 0]
    rows_block = destination.shape[0]
    lanes = jnp.arange(shard_total, dtype=jnp.int32)
    onehot = (destination[:, None] == lanes[None, :]).astype(jnp.int32)
    counts = lax.psum(jnp.sum(onehot.astype(jnp.float32), axis=0), "fsdp")
    row_weight = jnp.dot(
        onehot.astype(jnp.float32), float(rows_block) / counts, precision=lax.Precision.HIGHEST
    )
    rows_data = frames[0]
    action_rows = actions[0]
    fraction_rows = fractions[0]
    values = rows_data.astype(jnp.float32)
    mean_square = jnp.mean(values * values, axis=-1, keepdims=True)
    normed = (values * lax.rsqrt(mean_square + 1e-05) * norm_gain).astype(jnp.bfloat16)
    columns = normed
    preact = jnp.dot(
        columns,
        lax.all_gather(torso_weight, ("grp", "fsdp"), axis=0, tiled=True),
        preferred_element_type=jnp.float32,
    )
    choose_mask = (action_rows[:, None] == jnp.arange(ACTIONS, dtype=jnp.int32)[None, :]).astype(
        jnp.bfloat16
    )
    picked = jnp.dot(choose_mask, value_weight, preferred_element_type=jnp.float32)
    weighted = (jax.nn.silu(preact) * picked).astype(jnp.bfloat16)
    cosine = jnp.cos(
        jnp.pi * jnp.arange(COSINES, dtype=jnp.float32)[None, :] * table[:, None]
    ).astype(jnp.bfloat16)
    embedding = jax.nn.relu(
        jnp.dot(cosine, embed_weight, preferred_element_type=jnp.float32)
    ).astype(jnp.bfloat16)
    table_values = lax.dot_general(
        weighted, embedding, (((1,), (1,)), ((), ())), preferred_element_type=jnp.float32
    )
    selector = (
        fraction_rows[:, :, None] == jnp.arange(FRACS, dtype=jnp.int32)[None, None, :]
    ).astype(jnp.float32)
    partial_quant = jnp.einsum(
        "mj,mtj->mt", table_values, selector, precision=lax.Precision.HIGHEST
    )
    group_index = lax.axis_index("grp")
    own_slot = jnp.arange(2, dtype=jnp.int32)[:, None, None] == group_index
    stacked = jnp.where(
        own_slot, partial_quant[None, :, :], jnp.zeros_like(partial_quant)[None, :, :]
    )
    summed = lax.psum(stacked, ("grp", "tp"))
    target_quant = summed[0]
    online_quant = summed[1]
    learner = (group_index == 1).astype(jnp.float32)
    levels = jnp.einsum("mtj,j->mt", selector, table, precision=lax.Precision.HIGHEST)
    target_value = rewards.astype(jnp.float32)[:, None] + 0.99 * target_quant
    errors = target_value[:, None, :] - online_quant[:, :, None]
    weight = jnp.abs(levels[:, :, None] - (errors < 0).astype(jnp.float32))
    grad_quant = -(learner * row_weight)[:, None] * jnp.sum(
        weight * jnp.clip(errors, -1.0, 1.0), axis=-1
    )
    grad_table = jnp.einsum("mi,mij->mj", grad_quant, selector, precision=lax.Precision.HIGHEST)
    grad_feature = jnp.dot(
        grad_table, embedding.astype(jnp.float32), precision=lax.Precision.HIGHEST
    )
    gate_value = jax.nn.sigmoid(preact)
    grad_preact = (grad_feature * picked * gate_value * (1.0 + preact * (1.0 - gate_value))).astype(
        jnp.bfloat16
    )
    columns = normed
    torso_grad = lax.psum_scatter(
        lax.dot_general(
            columns, grad_preact, (((0,), (0,)), ((), ())), preferred_element_type=jnp.float32
        ),
        ("grp", "fsdp"),
        scatter_dimension=0,
        tiled=True,
    )
    updated = (torso_weight.astype(jnp.float32) - 0.01 * torso_grad).astype(jnp.bfloat16)
    refreshed_weight = lax.all_to_all(updated, "tp", split_axis=0, concat_axis=1, tiled=True)
    return (torso_grad, refreshed_weight)


def solution(mesh):
    placed = (
        P("grp", "fsdp", None),
        P("fsdp"),
        P("grp", "fsdp"),
        P("grp", "fsdp", None),
        P("fsdp", None),
        P(),
        P(),
        P(("grp", "fsdp"), "tp"),
        P(None, "tp"),
        P(None, "tp"),
    )
    return jax.shard_map(
        shards,
        mesh=mesh,
        in_specs=placed,
        out_specs=(P(("grp", "fsdp"), "tp"), P(("grp", "fsdp", "tp"), None)),
        check_vma=False,
    )
```

profile of v0, /device:TPU:1, one launch (start us, length us, event | category | flops | bytes accessed | tf_op | source)
XLA Modules:
  0.0 676.3 jit_solution(3532035005112224799)
XLA Ops:
  7.2 0.0 copy-start
  7.2 0.0 all-gather.2.cloned.1.call-start
  7.3 0.7 all-gather.2.cloned.1.call-update
  8.0 0.0 all-reduce.2.cloned.1.call-start
  8.0 0.8 convert_reduce_fusion
  8.8 39.0 %psum.14 = f32[16]{0:T(128)S(1)} all-reduce(f32[16]{0:T(128)S(1)} %convert_reduce_fusion), channel_id=1, replica_groups=mesh['grp'=2,'fsdp'=16,'tp'=8] {'fsdp'}, use_global_device_ids=true, to_apply=%region_2.0 | all-reduce | flops 16 | bytes 128 | tf_op jit(solution)/shard_map/psum | solution.py:28
  47.8 3.2 fusion
  51.0 0.1 fusion.25
  51.1 0.0 copy-done.5
  51.1 0.3 fusion.12
  51.5 0.3 fusion.19
  51.7 3.8 fusion.15
  55.5 27.9 %all-gather.2.cloned.1.call-done = bf16[8192,512]{1,0:T(8,128)(2,1)} async-done(((bf16[256,512]{1,0:T(8,128)(2,1)}), bf16[8192,512]{1,0:T(8,128)(2,1)}) %all-gather.2.cloned.1.call-update) | async-done | bytes 8388624 | tf_op jit(solution)/shard_map/all_gather | solution.py:41
  83.4 7.0 %fusion.10 = f32[256,512]{1,0:T(8,128)S(1)} fusion(bf16[8192,512]{1,0:T(8,128)(2,1)} %all-gather.2.cloned.1.call-done, bf16[1,256,8192]{2,1,0:T(8,128)(2,1)} %param.10, f32[8192]{0:T(1024)S(1)} %copy-done.3, f32[256]{0:T(256)S(1)} %add_rsqrt_fusion), kind=kOutput, calls=%fused_computation.17 | convolution fusion | flops 2155872256 | bytes 13140992 | tf_op jit(solution)/shard_map/dot_general | solution.py:39
  90.5 0.3 fusion.18
  90.8 0.4 select_reduce_fusion.1
  91.1 0.7 broadcast_select_fusion
  91.8 0.0 all-reduce.2.cloned.1.call-update
  91.9 0.0 reduce-scatter.2.cloned.1.call-start
  91.9 2.8 copy.17
  94.8 172.4 %all-reduce.2.cloned.1.call-done = f32[2,256,32]{1,2,0:T(8,128)} async-done(((f32[2,256,32]{1,2,0:T(8,128)}), f32[2,256,32]{1,2,0:T(8,128)}) %all-reduce.2.cloned.1.call-update) | async-done | bytes 65552 | tf_op jit(solution)/shard_map/psum | solution.py:69
  267.1 0.8 slice_bitcast_fusion
  267.9 0.8 fusion.22
  268.7 0.3 fusion.14
  269.0 0.4 select_reduce_fusion
  269.4 0.5 fusion.7
  270.0 10.4 %fusion.8 = f32[8192,512]{1,0:T(8,128)} fusion(bf16[256,512]{1,0:T(8,128)(2,1)S(1)} %fusion.7, bf16[1,256,8192]{2,1,0:T(8,128)(2,1)} %param.10, f32[8192]{0:T(1024)S(1)} %copy-done.3, f32[256]{0:T(256)S(1)} %add_rsqrt_fusion), kind=kOutput, calls=%fused_computation.16 | convolution fusion | flops 2155872256 | bytes 21267456 | tf_op jit(solution)/shard_map/dot_general | solution.py:90
  280.4 0.0 reduce-scatter.2.cloned.1.call-update
  280.4 370.4 %reduce-scatter.2.cloned.1.call-done = f32[256,512]{1,0:T(8,128)} async-done(((f32[8192,512]{1,0:T(8,128)}), f32[256,512]{1,0:T(8,128)}) %reduce-scatter.2.cloned.1.call-update) | async-done | bytes 524304 | tf_op jit(solution)/shard_map/reduce_scatter | solution.py:89
  650.8 1.1 subtract_convert_fusion
  651.9 17.1 %all_to_all.19 = bf16[8,32,512]{2,1,0:T(8,128)(2,1)S(1)} all-to-all(bf16[8,32,512]{2,1,0:T(8,128)(2,1)S(1)} %bitcast.39), channel_id=1, replica_groups=mesh['grp'=2,'fsdp'=16,'tp'=8] {'tp'}, dimensions={0} | all-to-all | bytes 524288 | tf_op jit(solution)/shard_map/all_to_all | solution.py:98
  669.0 0.7 copy.31
  (22 shorter events, 0.1 us)
Async XLA Ops:
  7.2 44.0 %copy-start = (bf16[64,512]{1,0:T(8,128)(2,1)S(1)}, bf16[64,512]{1,0:T(8,128)(2,1)}, u32[]{:S(2)}) copy-start(bf16[64,512]{1,0:T(8,128)(2,1)} %param.18) | copy-start | bytes 196612
  7.2 43.8 %copy-start.7 = (s32[256,1]{0,1:T(1,128)S(1)}, s32[256,1]{0,1:T(1,128)}, u32[]{:S(2)}) copy-start(s32[256,1]{0,1:T(1,128)} %param.14) | copy-start | bytes 3076
  7.2 43.9 %copy-start.5 = (f32[64]{0:T(128)S(1)}, f32[64]{0:T(128)}, u32[]{:S(2)}) copy-start(f32[64]{0:T(128)} %param.15) | copy-start | bytes 772
  7.2 44.2 %copy-start.4 = (bf16[18,512]{1,0:T(8,128)(2,1)S(1)}, bf16[18,512]{1,0:T(8,128)(2,1)}, u32[]{:S(2)}) copy-start(bf16[18,512]{1,0:T(8,128)(2,1)} %param.19) | copy-start | bytes 55300
  7.2 44.2 %copy-start.6 = (s32[1,256]{1,0:T(1,128)S(1)}, s32[1,256]{1,0:T(1,128)}, u32[]{:S(2)}) copy-start(s32[1,256]{1,0:T(1,128)} %param.12) | copy-start | bytes 3076
  7.2 44.5 %copy-start.2 = (s32[1,256,32]{1,2,0:T(8,128)S(1)}, s32[1,256,32]{1,2,0:T(8,128)}, u32[]{:S(2)}) copy-start(s32[1,256,32]{1,2,0:T(8,128)} %param.13) | copy-start | bytes 98308
  7.2 76.2 %all-gather.2.cloned.1.call-start = ((), (), s32[]{:S(2)}) async-start(), calls=%async_computation.2 | async-start | bytes 8650752 | tf_op jit(solution)/shard_map/all_gather | solution.py:41
  8.0 259.2 %all-reduce.2.cloned.1.call-start = ((), (), s32[]{:S(2)}) async-start(), calls=%async_computation.3 | async-start | bytes 131072 | tf_op jit(solution)/shard_map/psum | solution.py:69
  47.8 35.6 %copy-start.3 = (f32[8192]{0:T(1024)S(1)}, f32[8192]{0:T(1024)}, u32[]{:S(2)}) copy-start(f32[8192]{0:T(1024)} %param.16) | copy-start | bytes 98308
  55.5 36.4 %copy-start.8 = (bf16[256]{0:T(256)(128)(2,1)S(1)}, bf16[256]{0:T(256)(128)(2,1)}, u32[]{:S(2)}) copy-start(bf16[256]{0:T(256)(128)(2,1)} %param.11) | copy-start | bytes 1540
  91.9 558.9 %reduce-scatter.2.cloned.1.call-start = ((), (), s32[]{:S(2)}) async-start(), calls=%async_computation.4 | async-start | bytes 17301504 | tf_op jit(solution)/shard_map/reduce_scatter | solution.py:89
  280.4 370.4 %copy-start.1 = (bf16[256,512]{1,0:T(8,128)(2,1)S(1)}, bf16[256,512]{1,0:T(8,128)(2,1)}, u32[]{:S(2)}) copy-start(bf16[256,512]{1,0:T(8,128)(2,1)} %param.17) | copy-start | bytes 786436
Sparse Core Ops, SparseCore 0:
  9.9 73.4 all-gather.1
  92.0 175.1 all-reduce.1
  280.5 370.1 reduce-scatter.1
where the time goes:
time: 677 us; the launch traced here: 676 us
  waiting for transfers between devices  571 us (84%)
  blocking collectives  56.1 us (8%)
  matrix products  22.7 us (3%)
  between operations  13.9 us (2%)
  other arithmetic  7.65 us (1%)
    reduce_scatter x1, waiting for transfers between devices, shards(): lax.psum_scatter(lax.dot_general(columns, grad_preact, (((0,), (0,)), (()...  370 us
    psum x1, waiting for transfers between devices, shards(): summed = lax.psum(stacked, ('grp', 'tp'))  172 us
    psum x1, blocking collectives, shards(): counts = lax.psum(jnp.sum(onehot.astype(jnp.float32), axis=0), 'fsdp')  39 us
    all_gather x1, waiting for transfers between devices, shards(): lax.all_gather(torso_weight, ('grp', 'fsdp'), axis=0, tiled=True)  27.9 us
    all_to_all x1, blocking collectives, shards(): lax.all_to_all(updated, 'tp', split_axis=0, concat_axis=1, tiled=True)  17.1 us
  transfers between devices with their start and end apart: 3, of which 3 were waited for; matrix products, arithmetic and copies ran while one was open for 2% of the time, Pallas kernels for 0%

commit v1 on v0

--- a/solution.py
+++ b/solution.py
@@ -2,6 +2,7 @@
 import jax.numpy as jnp
 from jax import lax
 from jax.sharding import PartitionSpec as P
+from jax.lax import psum
 
 ACTIONS = 18
 COSINES = 64
@@ -66,7 +67,7 @@
     stacked = jnp.where(
         own_slot, partial_quant[None, :, :], jnp.zeros_like(partial_quant)[None, :, :]
     )
-    summed = lax.psum(stacked, ("grp", "tp"))
+    summed = psum(psum(stacked, "grp"), "tp")
     target_quant = summed[0]
     online_quant = summed[1]
     learner = (group_index == 1).astype(jnp.float32)

time: 677 us -> 632 us (0.934)
  waiting for transfers between devices: 571 us -> 527 us
    psum x1 -> x2, waiting for transfers between devices: 172 us -> 128 us  [shards(): summed = psum(psum(stacked, 'grp'), 'tp')]
  transfers between devices with their start and end apart: 3 -> 4, of which waited for: 3 -> 4; matrix products, arithmetic and copies ran while one was open for 2% -> 2% of each run, Pallas kernels for 0% -> 0%
where the time goes in v1:
time: 632 us
  waiting for transfers between devices  527 us (83%)
  blocking collectives  55.9 us (9%)
  matrix products  22.8 us (4%)
  between operations  13.9 us (2%)
  other arithmetic  7.65 us (1%)
    reduce_scatter x1, waiting for transfers between devices, shards(): lax.psum_scatter(lax.dot_general(columns, grad_preact, (((0,), (0,)), (()...  371 us
    psum x2, waiting for transfers between devices, shards(): summed = psum(psum(stacked, 'grp'), 'tp')  128 us
    psum x1, blocking collectives, shards(): counts = lax.psum(jnp.sum(onehot.astype(jnp.float32), axis=0), 'fsdp')  39 us
    all_gather x1, waiting for transfers between devices, shards(): lax.all_gather(torso_weight, ('grp', 'fsdp'), axis=0, tiled=True)  27.9 us
    all_to_all x1, blocking collectives, shards(): lax.all_to_all(updated, 'tp', split_axis=0, concat_axis=1, tiled=True)  16.8 us
  transfers between devices with their start and end apart: 4, of which 4 were waited for; matrix products, arithmetic and copies ran while one was open for 2% of the time, Pallas kernels for 0%

profile of v1, /device:TPU:1, one launch (start us, length us, event | category | flops | bytes accessed | tf_op | source)
XLA Modules:
  0.0 631.7 jit_solution(3746044577615661818)
XLA Ops:
  7.2 0.0 all-gather.2.cloned.1.call-start
  7.3 0.7 all-gather.2.cloned.1.call-update
  8.0 0.0 all-reduce.3.cloned.1.call-start
  8.0 0.8 convert_reduce_fusion
  8.8 39.0 %psum.21 = f32[16]{0:T(128)S(1)} all-reduce(f32[16]{0:T(128)S(1)} %convert_reduce_fusion), channel_id=1, replica_groups=mesh['grp'=2,'fsdp'=16,'tp'=8] {'fsdp'}, use_global_device_ids=true, to_apply=%region_2.0 | all-reduce | flops 16 | bytes 128 | tf_op jit(solution)/shard_map/psum | solution.py:29
  47.9 3.2 fusion
  51.0 0.3 fusion.12
  51.4 0.3 fusion.19
  51.7 3.8 fusion.15
  55.4 27.9 %all-gather.2.cloned.1.call-done = bf16[8192,512]{1,0:T(8,128)(2,1)} async-done(((bf16[256,512]{1,0:T(8,128)(2,1)}), bf16[8192,512]{1,0:T(8,128)(2,1)}) %all-gather.2.cloned.1.call-update) | async-done | bytes 8388624 | tf_op jit(solution)/shard_map/all_gather | solution.py:42
  83.4 7.0 %fusion.10 = f32[256,512]{1,0:T(8,128)S(1)} fusion(bf16[8192,512]{1,0:T(8,128)(2,1)} %all-gather.2.cloned.1.call-done, bf16[1,256,8192]{2,1,0:T(8,128)(2,1)} %param.10, f32[8192]{0:T(1024)S(1)} %copy-done.3, f32[256]{0:T(256)S(1)} %add_rsqrt_fusion), kind=kOutput, calls=%fused_computation.17 | convolution fusion | flops 2155872256 | bytes 13140992 | tf_op jit(solution)/shard_map/dot_general | solution.py:40
  90.4 0.3 fusion.18
  90.7 0.4 select_reduce_fusion.1
  91.1 0.7 broadcast_select_fusion
  91.8 0.0 all-reduce.3.cloned.1.call-update
  91.8 0.0 all-reduce.5.cloned.1.call-start
  91.9 0.1 fusion.25
  92.0 28.0 %all-reduce.3.cloned.1.call-done = f32[2,256,32]{1,2,0:T(8,128)} async-done(((f32[2,256,32]{1,2,0:T(8,128)}), f32[2,256,32]{1,2,0:T(8,128)}) %all-reduce.3.cloned.1.call-update) | async-done | bytes 65552 | tf_op jit(solution)/shard_map/psum | solution.py:70
  119.9 0.0 all-reduce.5.cloned.1.call-update
  120.0 0.0 reduce-scatter.2.cloned.1.call-start
  120.0 2.8 copy.17
  122.9 99.8 %all-reduce.5.cloned.1.call-done = f32[2,256,32]{1,2,0:T(8,128)} async-done(((f32[2,256,32]{1,2,0:T(8,128)}), f32[2,256,32]{1,2,0:T(8,128)}) %all-reduce.5.cloned.1.call-update) | async-done | bytes 65552 | tf_op jit(solution)/shard_map/psum | solution.py:70
  222.7 0.8 slice_bitcast_fusion
  223.5 0.8 fusion.22
  224.2 0.3 fusion.14
  224.6 0.4 select_reduce_fusion
  225.0 0.5 fusion.7
  225.5 10.4 %fusion.8 = f32[8192,512]{1,0:T(8,128)} fusion(bf16[256,512]{1,0:T(8,128)(2,1)S(1)} %fusion.7, bf16[1,256,8192]{2,1,0:T(8,128)(2,1)} %param.10, f32[8192]{0:T(1024)S(1)} %copy-done.3, f32[256]{0:T(256)S(1)} %add_rsqrt_fusion), kind=kOutput, calls=%fused_computation.16 | convolution fusion | flops 2155872256 | bytes 21267456 | tf_op jit(solution)/shard_map/dot_general | solution.py:91
  236.0 370.6 %reduce-scatter.2.cloned.1.call-done = f32[256,512]{1,0:T(8,128)} async-done(((f32[8192,512]{1,0:T(8,128)}), f32[256,512]{1,0:T(8,128)}) %reduce-scatter.2.cloned.1.call-update) | async-done | bytes 524304 | tf_op jit(solution)/shard_map/reduce_scatter | solution.py:90
  606.5 1.1 subtract_convert_fusion
  607.6 16.8 %all_to_all.19 = bf16[8,32,512]{2,1,0:T(8,128)(2,1)S(1)} all-to-all(bf16[8,32,512]{2,1,0:T(8,128)(2,1)S(1)} %bitcast.39), channel_id=1, replica_groups=mesh['grp'=2,'fsdp'=16,'tp'=8] {'tp'}, dimensions={0} | all-to-all | bytes 524288 | tf_op jit(solution)/shard_map/all_to_all | solution.py:99
  624.5 0.7 copy.31
  (25 shorter events, 0.1 us)
Async XLA Ops:
  7.2 43.9 %copy-start = (bf16[64,512]{1,0:T(8,128)(2,1)S(1)}, bf16[64,512]{1,0:T(8,128)(2,1)}, u32[]{:S(2)}) copy-start(bf16[64,512]{1,0:T(8,128)(2,1)} %param.18) | copy-start | bytes 196612
  7.2 43.9 %copy-start.5 = (f32[64]{0:T(128)S(1)}, f32[64]{0:T(128)}, u32[]{:S(2)}) copy-start(f32[64]{0:T(128)} %param.15) | copy-start | bytes 772
  7.2 44.2 %copy-start.4 = (bf16[18,512]{1,0:T(8,128)(2,1)S(1)}, bf16[18,512]{1,0:T(8,128)(2,1)}, u32[]{:S(2)}) copy-start(bf16[18,512]{1,0:T(8,128)(2,1)} %param.19) | copy-start | bytes 55300
  7.2 44.2 %copy-start.6 = (s32[1,256]{1,0:T(1,128)S(1)}, s32[1,256]{1,0:T(1,128)}, u32[]{:S(2)}) copy-start(s32[1,256]{1,0:T(1,128)} %param.12) | copy-start | bytes 3076
  7.2 44.4 %copy-start.2 = (s32[1,256,32]{1,2,0:T(8,128)S(1)}, s32[1,256,32]{1,2,0:T(8,128)}, u32[]{:S(2)}) copy-start(s32[1,256,32]{1,2,0:T(8,128)} %param.13) | copy-start | bytes 98308
  7.2 76.2 %all-gather.2.cloned.1.call-start = ((), (), s32[]{:S(2)}) async-start(), calls=%async_computation.2 | async-start | bytes 8650752 | tf_op jit(solution)/shard_map/all_gather | solution.py:42
  8.0 112.0 %all-reduce.3.cloned.1.call-start = ((), (), s32[]{:S(2)}) async-start(), calls=%async_computation.3 | async-start | bytes 131072 | tf_op jit(solution)/shard_map/psum | solution.py:70
  47.9 35.5 %copy-start.3 = (f32[8192]{0:T(1024)S(1)}, f32[8192]{0:T(1024)}, u32[]{:S(2)}) copy-start(f32[8192]{0:T(1024)} %param.16) | copy-start | bytes 98308
  55.4 36.4 %copy-start.7 = (s32[256,1]{0,1:T(1,128)S(1)}, s32[256,1]{0,1:T(1,128)}, u32[]{:S(2)}) copy-start(s32[256,1]{0,1:T(1,128)} %param.14) | copy-start | bytes 3076
  55.4 64.6 %copy-start.8 = (bf16[256]{0:T(256)(128)(2,1)S(1)}, bf16[256]{0:T(256)(128)(2,1)}, u32[]{:S(2)}) copy-start(bf16[256]{0:T(256)(128)(2,1)} %param.11) | copy-start | bytes 1540
  91.8 130.9 %all-reduce.5.cloned.1.call-start = ((), (), s32[]{:S(2)}) async-start(), calls=%async_computation.4 | async-start | bytes 131072 | tf_op jit(solution)/shard_map/psum | solution.py:70
  120.0 486.6 %reduce-scatter.2.cloned.1.call-start = ((), (), s32[]{:S(2)}) async-start(), calls=%async_computation.5 | async-start | bytes 17301504 | tf_op jit(solution)/shard_map/reduce_scatter | solution.py:90
  235.9 370.6 %copy-start.1 = (bf16[256,512]{1,0:T(8,128)(2,1)S(1)}, bf16[256,512]{1,0:T(8,128)(2,1)}, u32[]{:S(2)}) copy-start(bf16[256,512]{1,0:T(8,128)(2,1)} %param.17) | copy-start | bytes 786436
Sparse Core Ops, SparseCore 0:
  9.9 73.4 all-gather.1
  91.9 27.9 all-reduce.2
  122.5 100.1 all-reduce.4
  236.1 370.3 reduce-scatter.1
